TPU v7x, 256 devices: a whole 4x4x8 slice. The times are simulated.
256 devices in a mesh: lat: 16 (over z, core), lon: 16 (over y, x).
Axes of the slice: x: 4, y: 4, z: 8, core: 2. Of those that a mesh axis runs over, the one named last changes fastest.
Arguments:
- density: float32 [75, 256, 4096], P(None, 'lat', 'lon'), may hold values from -24 to 24
- tend_east: float32 [75, 256, 4096], P(None, 'lat', 'lon'), may hold values from -6 to 6
- tend_north: float32 [75, 256, 4096], P(None, 'lat', 'lon'), may hold values from -6 to 6
- thickness: float32 [75], replicated, may hold values from 0.02 to 0.2
- levels: int32 [256, 4096], P('lat', 'lon'), may hold values from 1 to 75
- ocean_mask: int32 [256, 4096], P('lat', 'lon'), may hold values 0 or 1
- eta_prev: float32 [256, 4096], P('lat', 'lon'), may hold values from -1.2 to 1.2
- coarse: float32 [4096, 4096], P(('lat', 'lon')), as said below
Outputs:
- surface: float32 [256, 4096], P('lat', 'lon')
- precond_residual: float32 [256, 4096], P('lat', 'lon')
Inputs may be any that keep to these rules, and one draw needn't show every extreme that they name: coarse is symmetric positive definite.
All inputs are finite; a program needn't handle non-finite values. No bound on the sum of `ocean_mask` on one device may be relied on, other than what follows from the above.
Results may differ from a plain program's by a relative error of at most 0.0003.
Values sent between devices are 32-bit elements; how exact they have to be, the bound alone decides.
No kernel may reach another device: no remote copies, remote signals or barrier semaphores. Data moves between devices by JAX's collectives and lax.ppermute only.
A program may use at most 64 MiB of HBM per device.

v0:
```python
import jax
import jax.numpy as jnp
from jax import lax
from jax.sharding import PartitionSpec as P

K = 75
TILE_SIDE = 4
ITERS = 2
surface_coeff = 0.25
highest = lax.Precision.HIGHEST


def with_halo(shard, sides, width):
    for axis, dim in sides:
        peers, length = (lax.axis_size(axis), shard.shape[dim])
        up = [(i, (i + 1) % peers) for i in range(peers)]
        down = [(j, i) for i, j in up]
        last = lax.slice_in_dim(shard, length - width, length, axis=dim)
        leading = lax.slice_in_dim(shard, 0, width, axis=dim)
        before = lax.ppermute(last, axis, up)
        after = lax.ppermute(leading, axis, down)
        shard = jnp.concatenate([before, shard, after], axis=dim)
    return shard


def wall_rows(framed, rim_width):
    row_count = framed.shape[1]
    row_index = lax.broadcasted_iota(jnp.int32, (1, row_count, 1), 1)
    position = lax.axis_index("lat")
    last_index = lax.axis_size("lat") - 1
    southern = jnp.logical_and(position == 0, row_index < rim_width)
    northern = jnp.logical_and(position == last_index, row_index >= row_count - rim_width)
    return jnp.where(jnp.logical_or(southern, northern), 0.0, framed)


def plane_halo(planes):
    return wall_rows(with_halo(planes, (("lat", 1), ("lon", 2)), 1), 1)


def global_sum(partial_value):
    return lax.psum(partial_value, ("lat", "lon"))


def gather_coarse(own_values):
    return lax.all_gather(own_values, ("lat", "lon"), axis=0, tiled=True)


def restrict_local(values, ocean_share):
    tile_rows = values.shape[0] // TILE_SIDE
    tile_cols = values.shape[1] // TILE_SIDE
    tiled_sum = (values * ocean_share).reshape(TILE_SIDE, tile_rows, TILE_SIDE, tile_cols)
    return jnp.sum(tiled_sum, axis=(1, 3)).reshape(-1)


def prolong_local(coarse_values, ocean_share):
    tile_rows = ocean_share.shape[0] // TILE_SIDE
    tile_cols = ocean_share.shape[1] // TILE_SIDE
    blocks = coarse_values.reshape(TILE_SIDE, 1, TILE_SIDE, 1)
    spread = jnp.broadcast_to(blocks, (TILE_SIDE, tile_rows, TILE_SIDE, tile_cols))
    return spread.reshape(ocean_share.shape) * ocean_share


def east_fourth(own_rows):
    return (
        8.0 * (own_rows[:, :, 3:-1] - own_rows[:, :, 1:-3])
        - (own_rows[:, :, 4:] - own_rows[:, :, :-4])
    ) / 12.0


def north_fourth(own_cols):
    return (
        8.0 * (own_cols[:, 3:-1, :] - own_cols[:, 1:-3, :])
        - (own_cols[:, 4:, :] - own_cols[:, :-4, :])
    ) / 12.0


def apply_operator(face_list, diagonal, values, beside_all):
    east_face, west_face, north_face, south_face = face_list
    return diagonal * values - (
        east_face * beside_all[1:-1, 2:]
        + west_face * beside_all[1:-1, :-2]
        + north_face * beside_all[2:, 1:-1]
        + south_face * beside_all[:-2, 1:-1]
    )


def body(density, tend_east, tend_north, thickness, levels, ocean_mask, eta_prev, coarse):
    wet_levels = levels * ocean_mask
    ocean_share = ocean_mask.astype(jnp.float32)
    layer_weight = thickness[:, None, None]
    depth_index = lax.broadcasted_iota(jnp.int32, (K,) + wet_levels.shape, 0)
    active = (depth_index < wet_levels[None]).astype(jnp.float32)
    lower_ones = (
        lax.broadcasted_iota(jnp.int32, (K, K), 1) <= lax.broadcasted_iota(jnp.int32, (K, K), 0)
    ).astype(jnp.float32)
    pressure = (
        jnp.einsum("kj,jab->kab", lower_ones, layer_weight * density, precision=highest) * active
    )
    solution = ocean_share * eta_prev
    framed = wall_rows(with_halo(pressure, (("lat", 1), ("lon", 2)), 2), 2)
    east_diff = east_fourth(framed[:, 2:-2, :])
    north_diff = north_fourth(framed[:, :, 2:-2])
    force_east = jnp.sum(layer_weight * active * (tend_east - east_diff), axis=0)
    force_north = jnp.sum(layer_weight * active * (tend_north - north_diff), axis=0)
    column_depth = jnp.sum(layer_weight * active, axis=0)
    planes = plane_halo(jnp.stack([force_east, force_north, column_depth, solution]))
    right_side = (
        ocean_share
        * 0.5
        * (planes[0, 1:-1, :-2] - planes[0, 1:-1, 2:] + planes[1, :-2, 1:-1] - planes[1, 2:, 1:-1])
    )
    depth_framed = planes[2]
    solution_framed = planes[3]
    center = depth_framed[1:-1, 1:-1]
    face_list = (
        jnp.minimum(center, depth_framed[1:-1, 2:]),
        jnp.minimum(center, depth_framed[1:-1, :-2]),
        jnp.minimum(center, depth_framed[2:, 1:-1]),
        jnp.minimum(center, depth_framed[:-2, 1:-1]),
    )
    diagonal = ocean_share * (
        surface_coeff + face_list[0] + face_list[1] + face_list[2] + face_list[3]
    ) + (1.0 - ocean_share)

    def precondition(values):
        coarse_all = gather_coarse(restrict_local(values, ocean_share))
        return values / diagonal + prolong_local(
            jnp.dot(coarse, coarse_all, precision=highest), ocean_share
        )

    residual = right_side - apply_operator(face_list, diagonal, solution, solution_framed)
    precond = precondition(residual)
    direction = precond
    rz_now = global_sum(jnp.sum(residual * precond))
    for iteration in range(ITERS):
        beside_all = plane_halo(direction[None])[0]
        image_field = apply_operator(face_list, diagonal, direction, beside_all)
        step_length = rz_now / global_sum(jnp.sum(direction * image_field))
        solution = solution + step_length * direction
        residual = residual - step_length * image_field
        precond = precondition(residual)
        if iteration + 1 < ITERS:
            rz_next = global_sum(jnp.sum(residual * precond))
            direction = precond + rz_next / rz_now * direction
            rz_now = rz_next
    return (solution, precond)


def solution(mesh):
    return jax.shard_map(
        body,
        mesh=mesh,
        in_specs=(
            P(None, "lat", "lon"),
            P(None, "lat", "lon"),
            P(None, "lat", "lon"),
            P(),
            P("lat", "lon"),
            P("lat", "lon"),
            P("lat", "lon"),
            P(("lat", "lon"), None),
        ),
        out_specs=(P("lat", "lon"), P("lat", "lon")),
        check_vma=False,
    )
```

profile of v0, /device:TPU:1, one launch (start us, length us, event | category | flops | bytes accessed | tf_op | source)
XLA Modules:
  0.0 525.2 jit_solution(2610545018374523092)
XLA Ops:
  0.6 0.8 mul.159
  2.0 2.8 convolution_select_fusion
  4.9 3.0 collective-permute-start
  8.8 1.4 collective-permute-done
  10.2 2.8 collective-permute-done.1
  13.4 0.9 copy.25
  14.3 1.2 collective-permute-start.2
  15.8 3.8 collective-permute-start.3
  21.0 1.1 copy.28
  22.2 1.7 maximum_select_fusion
  23.9 2.6 fusion
  26.6 0.7 collective-permute-start.4
  27.3 2.1 collective-permute-start.5
  30.5 5.0 collective-permute-start.7
  35.5 1.4 collective-permute-done.6
  37.6 82.0 %all-reduce = f32[4096]{0:T(1024)S(1)} all-reduce(f32[4096]{0:T(1024)S(1)} %dynamic-update-slice), channel_id=1, replica_groups=mesh['lat'=16,'lon'=16] {'lat','lon'}, use_global_device_ids=true, to_apply=%add | all-reduce | flops 4096 | bytes 32768
  120.4 1.0 collective-permute-start.9
  122.0 1.4 collective-permute-done.9
  123.5 4.8 collective-permute-start.11
  128.3 1.1 collective-permute-done.10
  129.5 0.7 multiply_reduce_fusion.2
  130.2 79.6 %all-reduce.3 = (f32[]{:T(128)}, f32[]{:T(128)}) all-reduce(f32[]{:T(128)} %get-tuple-element.6, f32[]{:T(128)} %get-tuple-element.5), channel_id=1, replica_groups=mesh['lat'=16,'lon'=16] {'lat','lon'}, use_global_device_ids=true, to_apply=%region_5.6 | all-reduce | flops 2 | bytes 16 | tf_op jit(solution)/shard_map/psum | solution.py:41
  211.6 72.8 %all-reduce.1 = f32[4096]{0:T(1024)S(1)} all-reduce(f32[4096]{0:T(1024)S(1)} %dynamic-update-slice.1), channel_id=1, replica_groups=mesh['lat'=16,'lon'=16] {'lat','lon'}, use_global_device_ids=true, to_apply=%add.1 | all-reduce | flops 4096 | bytes 32768
  285.7 73.5 %psum.30 = f32[]{:T(128)} all-reduce(f32[]{:T(128)} %multiply_reduce_fusion.1), channel_id=1, replica_groups=mesh['lat'=16,'lon'=16] {'lat','lon'}, use_global_device_ids=true, to_apply=%region_10.11 | all-reduce | flops 1 | bytes 8 | tf_op jit(solution)/shard_map/psum | solution.py:41
  360.5 1.5 collective-permute-start.12
  362.0 0.7 collective-permute-done.12
  362.8 2.3 collective-permute-done.13
  365.1 0.7 collective-permute-start.14
  365.8 4.1 collective-permute-start.15
  369.9 1.1 collective-permute-done.14
  371.8 77.7 %psum.31 = f32[]{:T(128)} all-reduce(f32[]{:T(128)} %get-tuple-element.9), channel_id=1, replica_groups=mesh['lat'=16,'lon'=16] {'lat','lon'}, use_global_device_ids=true, to_apply=%region_12.13 | all-reduce | flops 1 | bytes 8 | tf_op jit(solution)/shard_map/psum | solution.py:41
  451.3 72.6 %all-reduce.2 = f32[4096]{0:T(1024)S(1)} all-reduce(f32[4096]{0:T(1024)S(1)} %dynamic-update-slice.2), channel_id=1, replica_groups=mesh['lat'=16,'lon'=16] {'lat','lon'}, use_global_device_ids=true, to_apply=%add.2 | all-reduce | flops 4096 | bytes 32768
  (89 shorter events, 11.4 us)
Async XLA Ops:
  0.6 119.0 %copy-start = (f32[16,4096]{1,0:T(8,128)S(1)}, f32[16,4096]{1,0:T(8,128)}, u32[]{:S(2)}) copy-start(f32[16,4096]{1,0:T(8,128)} %param.15) | copy-start | bytes 786436
  1.4 0.6 copy-start.5
  2.0 6.1 %copy-start.1 = (s32[16,256]{1,0:T(8,128)S(1)}, s32[16,256]{1,0:T(8,128)}, u32[]{:S(2)}) copy-start(s32[16,256]{1,0:T(8,128)} %param.13) | copy-start | bytes 49156
  2.0 6.1 %copy-start.7 = (f32[16,256]{1,0:T(8,128)S(1)}, f32[16,256]{1,0:T(8,128)}, u32[]{:S(2)}) copy-start(f32[16,256]{1,0:T(8,128)} %param.14) | copy-start | bytes 49156
  4.9 5.3 %collective-permute-start = (f32[75,2,256]{2,0,1:T(8,128)S(1)}, f32[75,2,256]{2,0,1:T(8,128)S(1)}, u32[]{:S(2)}, u32[]{:S(2)}) collective-permute-start(f32[75,2,256]{2,0,1:T(8,128)S(1)} %get-tuple-element.23), channel_id=1, source_target_pairs={{0,16},{16,32},{32,48},{48,64},{64,80},{80,96},{96,112},{112,128},... | collective-permute-start | bytes 460808 | tf_op jit(solution)/shard_map/ppermute | solution.py:20
  7.9 5.0 collective-permute-start.1
  14.3 6.3 %collective-permute-start.2 = (f32[75,20,2]{0,2,1:T(2,128)}, f32[75,20,2]{0,2,1:T(2,128)S(1)}, u32[]{:S(2)}, u32[]{:S(2)}) collective-permute-start(f32[75,20,2]{0,2,1:T(2,128)} %copy.25), channel_id=1, source_target_pairs={{0,1},{1,2},{2,3},{3,4},{4,5},{5,6},{6,7},{7,8},{8,9},{9,10},{10,1... | collective-permute-start | bytes 36008 | tf_op jit(solution)/shard_map/ppermute | solution.py:20
  15.8 5.2 collective-permute-start.3
  22.1 1.8 copy-start.2
  22.1 1.8 copy-start.3
  22.1 1.8 copy-start.6
  22.1 1.8 copy-start.9
  23.9 2.6 copy-start.4
  23.9 13.1 %copy-start.8 = (f32[16,256]{1,0:T(8,128)S(1)}, f32[16,256]{1,0:T(8,128)}, u32[]{:S(2)}) copy-start(f32[16,256]{1,0:T(8,128)} %param.14) | copy-start | bytes 49156
  26.6 3.4 collective-permute-start.4
  27.3 3.0 collective-permute-start.5
  30.4 6.4 %collective-permute-start.6 = (f32[4,18,1]{2,1,0:T(8,128)S(1)}, f32[4,18,1]{2,1,0:T(8,128)S(1)}, u32[]{:S(2)}, u32[]{:S(2)}) collective-permute-start(f32[4,18,1]{2,1,0:T(8,128)S(1)} %get-tuple-element.27), channel_id=1, source_target_pairs={{0,1},{1,2},{2,3},{3,4},{4,5},{5,6},{6,7},{7,8},{8,9},{9,10},{10,1... | collective-permute-start | bytes 872 | tf_op jit(solution)/shard_map/ppermute | solution.py:20
  30.5 6.4 %collective-permute-start.7 = (f32[4,18,1]{2,1,0:T(8,128)S(1)}, f32[4,18,1]{2,1,0:T(8,128)S(1)}, u32[]{:S(2)}, u32[]{:S(2)}) collective-permute-start(f32[4,18,1]{2,1,0:T(8,128)S(1)} %get-tuple-element.28), channel_id=1, source_target_pairs={{1,0},{2,1},{3,2},{4,3},{5,4},{6,5},{7,6},{8,7},{9,8},{10,9},{11,1... | collective-permute-start | bytes 872 | tf_op jit(solution)/shard_map/ppermute | solution.py:21
  120.4 1.7 collective-permute-start.8
  120.4 3.0 collective-permute-start.9
  123.5 5.9 %collective-permute-start.10 = (f32[1,18,1]{2,1,0:T(8,128)S(1)}, f32[1,18,1]{2,1,0:T(8,128)S(1)}, u32[]{:S(2)}, u32[]{:S(2)}) collective-permute-start(f32[1,18,1]{2,1,0:T(8,128)S(1)} %get-tuple-element.33), channel_id=1, source_target_pairs={{0,1},{1,2},{2,3},{3,4},{4,5},{5,6},{6,7},{7,8},{8,9},{9,10},{10,1... | collective-permute-start | bytes 224 | tf_op jit(solution)/shard_map/ppermute | solution.py:20
  123.5 5.9 %collective-permute-start.11 = (f32[1,18,1]{2,1,0:T(8,128)S(1)}, f32[1,18,1]{2,1,0:T(8,128)S(1)}, u32[]{:S(2)}, u32[]{:S(2)}) collective-permute-start(f32[1,18,1]{2,1,0:T(8,128)S(1)} %get-tuple-element.34), channel_id=1, source_target_pairs={{1,0},{2,1},{3,2},{4,3},{5,4},{6,5},{7,6},{8,7},{9,8},{10,9},{11,1... | collective-permute-start | bytes 224 | tf_op jit(solution)/shard_map/ppermute | solution.py:21
  360.5 2.3 collective-permute-start.12
  362.0 3.0 collective-permute-start.13
  365.1 5.9 %collective-permute-start.14 = (f32[1,18,1]{2,1,0:T(8,128)S(1)}, f32[1,18,1]{2,1,0:T(8,128)S(1)}, u32[]{:S(2)}, u32[]{:S(2)}) collective-permute-start(f32[1,18,1]{2,1,0:T(8,128)S(1)} %get-tuple-element.31), channel_id=1, source_target_pairs={{0,1},{1,2},{2,3},{3,4},{4,5},{5,6},{6,7},{7,8},{8,9},{9,10},{10,1... | collective-permute-start | bytes 224 | tf_op jit(solution)/shard_map/ppermute | solution.py:20
  365.8 5.2 collective-permute-start.15
where the time goes:
time: 527 us; the launch traced here: 525 us
  blocking collectives  458 us (87%)
  starting transfers between devices  28.2 us (5%)
  waiting for transfers between devices  14.2 us (3%)
  other arithmetic  9.79 us (2%)
  local copies, waits for them, and re-layouts  5.91 us (1%)
    psum x3, blocking collectives, global_sum(): return lax.psum(partial_value, ('lat', 'lon'))  231 us
    unnamed x3, blocking collectives  227 us
    ppermute x8, starting transfers between devices, with_halo(): after = lax.ppermute(leading, axis, down)  20.9 us
  transfers between devices with their start and end apart: 16, of which 12 were waited for; matrix products, arithmetic and copies ran while one was open for 0% of the time, Pallas kernels for 0%

commit v1 on v0

--- a/solution.py
+++ b/solution.py
@@ -38,7 +38,7 @@
 
 
 def global_sum(partial_value):
-    return lax.psum(partial_value, ("lat", "lon"))
+    return lax.psum(lax.psum(partial_value, "lon"), "lat")
 
 
 def gather_coarse(own_values):

time: 527 us -> 492 us (0.934)
  blocking collectives: 458 us -> 426 us
    psum x3 -> x6, blocking collectives: 231 us -> 198 us  [global_sum(): return lax.psum(lax.psum(partial_value, 'lon'), 'lat')]
where the time goes in v1:
time: 492 us; the launch traced here: 491 us
  blocking collectives  426 us (87%)
  starting transfers between devices  27.4 us (6%)
  waiting for transfers between devices  13.5 us (3%)
  other arithmetic  9.79 us (2%)
  local copies, waits for them, and re-layouts  5.91 us (1%)
  between operations  4.96 us (1%)
    unnamed x3, blocking collectives  228 us
    psum x6, blocking collectives, global_sum(): return lax.psum(lax.psum(partial_value, 'lon'), 'lat')  198 us
    ppermute x8, starting transfers between devices, with_halo(): after = lax.ppermute(leading, axis, down)  21.8 us
  transfers between devices with their start and end apart: 16, of which 12 were waited for; matrix products, arithmetic and copies ran while one was open for 0% of the time, Pallas kernels for 0%

profile of v1, /device:TPU:1, one launch (start us, length us, event | category | flops | bytes accessed | tf_op | source)
XLA Modules:
  0.0 491.2 jit_solution(8075738755638618896)
XLA Ops:
  0.6 0.8 mul.159
  2.0 2.8 convolution_select_fusion
  4.9 3.0 collective-permute-start
  8.8 1.4 collective-permute-done
  10.2 2.8 collective-permute-done.1
  13.4 0.9 copy.25
  14.3 1.2 collective-permute-start.2
  15.8 3.8 collective-permute-start.3
  21.0 1.1 copy.28
  22.2 1.7 maximum_select_fusion
  23.9 2.6 fusion
  26.6 0.7 collective-permute-start.4
  27.3 2.1 collective-permute-start.5
  30.5 5.0 %collective-permute-start.7 = (f32[4,18,1]{2,1,0:T(8,128)S(1)}, f32[4,18,1]{2,1,0:T(8,128)S(1)}, u32[]{:S(2)}, u32[]{:S(2)}) collective-permute-start(f32[4,18,1]{2,1,0:T(8,128)S(1)} %get-tuple-element.30), channel_id=1, source_target_pairs={{1,0},{2,1},{3,2},{4,3},{5,4},{6,5},{7,6},{8,7},{9,8},{10,9},{11,1... | collective-permute-start | bytes 872 | tf_op jit(solution)/shard_map/ppermute | solution.py:21
  35.5 1.4 collective-permute-done.6
  37.6 82.0 %all-reduce = f32[4096]{0:T(1024)S(1)} all-reduce(f32[4096]{0:T(1024)S(1)} %dynamic-update-slice), channel_id=1, replica_groups=mesh['lat'=16,'lon'=16] {'lat','lon'}, use_global_device_ids=true, to_apply=%add | all-reduce | flops 4096 | bytes 32768
  120.4 1.0 collective-permute-start.9
  122.0 1.4 collective-permute-done.9
  123.5 4.8 collective-permute-start.11
  128.3 1.1 collective-permute-done.10
  129.5 0.7 multiply_reduce_fusion.2
  130.2 34.2 %all-reduce.3 = (f32[]{:T(128)}, f32[]{:T(128)}) all-reduce(f32[]{:T(128)} %get-tuple-element.6, f32[]{:T(128)} %get-tuple-element.5), channel_id=1, replica_groups=mesh['lat'=16,'lon'=16] {'lon'}, use_global_device_ids=true, to_apply=%region_5.6 | all-reduce | flops 2 | bytes 16 | tf_op jit(solution)/shard_map/psum | solution.py:41
  164.3 34.2 %all-reduce.4 = (f32[]{:T(128)}, f32[]{:T(128)}) all-reduce(f32[]{:T(128)} %get-tuple-element.7, f32[]{:T(128)} %get-tuple-element.8), channel_id=1, replica_groups=mesh['lat'=16,'lon'=16] {'lat'}, use_global_device_ids=true, to_apply=%region_6.7 | all-reduce | flops 2 | bytes 16 | tf_op jit(solution)/shard_map/psum | solution.py:41
  200.3 72.8 %all-reduce.1 = f32[4096]{0:T(1024)S(1)} all-reduce(f32[4096]{0:T(1024)S(1)} %dynamic-update-slice.1), channel_id=1, replica_groups=mesh['lat'=16,'lon'=16] {'lat','lon'}, use_global_device_ids=true, to_apply=%add.1 | all-reduce | flops 4096 | bytes 32768
  274.4 30.3 %psum.60 = f32[]{:T(128)} all-reduce(f32[]{:T(128)} %multiply_reduce_fusion.1), channel_id=1, replica_groups=mesh['lat'=16,'lon'=16] {'lon'}, use_global_device_ids=true, to_apply=%region_12.13 | all-reduce | flops 1 | bytes 8 | tf_op jit(solution)/shard_map/psum | solution.py:41
  304.7 31.5 %psum.61 = f32[]{:T(128)} all-reduce(f32[]{:T(128)} %psum.60), channel_id=1, replica_groups=mesh['lat'=16,'lon'=16] {'lat'}, use_global_device_ids=true, to_apply=%region_13.14 | all-reduce | flops 1 | bytes 8 | tf_op jit(solution)/shard_map/psum | solution.py:41
  338.8 1.7 collective-permute-done.13
  341.2 4.3 collective-permute-start.15
  345.4 1.1 collective-permute-done.14
  347.3 33.9 %psum.62 = f32[]{:T(128)} all-reduce(f32[]{:T(128)} %get-tuple-element.11), channel_id=1, replica_groups=mesh['lat'=16,'lon'=16] {'lon'}, use_global_device_ids=true, to_apply=%region_15.16 | all-reduce | flops 1 | bytes 8 | tf_op jit(solution)/shard_map/psum | solution.py:41
  381.2 34.0 %psum.63 = f32[]{:T(128)} all-reduce(f32[]{:T(128)} %psum.62), channel_id=1, replica_groups=mesh['lat'=16,'lon'=16] {'lat'}, use_global_device_ids=true, to_apply=%region_16.17 | all-reduce | flops 1 | bytes 8 | tf_op jit(solution)/shard_map/psum | solution.py:41
  417.1 72.8 %all-reduce.2 = f32[4096]{0:T(1024)S(1)} all-reduce(f32[4096]{0:T(1024)S(1)} %dynamic-update-slice.2), channel_id=1, replica_groups=mesh['lat'=16,'lon'=16] {'lat','lon'}, use_global_device_ids=true, to_apply=%add.2 | all-reduce | flops 4096 | bytes 32768
  (92 shorter events, 13.3 us)
Async XLA Ops:
  0.6 119.0 %copy-start = (f32[16,4096]{1,0:T(8,128)S(1)}, f32[16,4096]{1,0:T(8,128)}, u32[]{:S(2)}) copy-start(f32[16,4096]{1,0:T(8,128)} %param.15) | copy-start | bytes 786436
  1.4 0.6 copy-start.5
  2.0 6.1 %copy-start.1 = (s32[16,256]{1,0:T(8,128)S(1)}, s32[16,256]{1,0:T(8,128)}, u32[]{:S(2)}) copy-start(s32[16,256]{1,0:T(8,128)} %param.13) | copy-start | bytes 49156
  2.0 6.1 %copy-start.7 = (f32[16,256]{1,0:T(8,128)S(1)}, f32[16,256]{1,0:T(8,128)}, u32[]{:S(2)}) copy-start(f32[16,256]{1,0:T(8,128)} %param.14) | copy-start | bytes 49156
  4.9 5.3 %collective-permute-start = (f32[75,2,256]{2,0,1:T(8,128)S(1)}, f32[75,2,256]{2,0,1:T(8,128)S(1)}, u32[]{:S(2)}, u32[]{:S(2)}) collective-permute-start(f32[75,2,256]{2,0,1:T(8,128)S(1)} %get-tuple-element.25), channel_id=1, source_target_pairs={{0,16},{16,32},{32,48},{48,64},{64,80},{80,96},{96,112},{112,128},... | collective-permute-start | bytes 460808 | tf_op jit(solution)/shard_map/ppermute | solution.py:20
  7.9 5.0 %collective-permute-start.1 = (f32[75,2,256]{2,0,1:T(8,128)S(1)}, f32[75,2,256]{2,0,1:T(8,128)S(1)}, u32[]{:S(2)}, u32[]{:S(2)}) collective-permute-start(f32[75,2,256]{2,0,1:T(8,128)S(1)} %get-tuple-element.26), channel_id=1, source_target_pairs={{16,0},{32,16},{48,32},{64,48},{80,64},{96,80},{112,96},{128,112},... | collective-permute-start | bytes 460808 | tf_op jit(solution)/shard_map/ppermute | solution.py:21
  14.3 6.3 %collective-permute-start.2 = (f32[75,20,2]{0,2,1:T(2,128)}, f32[75,20,2]{0,2,1:T(2,128)S(1)}, u32[]{:S(2)}, u32[]{:S(2)}) collective-permute-start(f32[75,20,2]{0,2,1:T(2,128)} %copy.25), channel_id=1, source_target_pairs={{0,1},{1,2},{2,3},{3,4},{4,5},{5,6},{6,7},{7,8},{8,9},{9,10},{10,1... | collective-permute-start | bytes 36008 | tf_op jit(solution)/shard_map/ppermute | solution.py:20
  15.8 5.2 %collective-permute-start.3 = (f32[75,20,2]{0,2,1:T(2,128)S(1)}, f32[75,20,2]{0,2,1:T(2,128)}, u32[]{:S(2)}, u32[]{:S(2)}) collective-permute-start(f32[75,20,2]{0,2,1:T(2,128)S(1)} %copy.26), channel_id=1, source_target_pairs={{1,0},{2,1},{3,2},{4,3},{5,4},{6,5},{7,6},{8,7},{9,8},{10,9},{11,1... | collective-permute-start | bytes 36008 | tf_op jit(solution)/shard_map/ppermute | solution.py:21
  22.1 1.8 copy-start.2
  22.1 1.8 copy-start.3
  22.1 1.8 copy-start.6
  22.1 1.8 copy-start.9
  23.9 2.6 copy-start.4
  23.9 13.1 %copy-start.8 = (f32[16,256]{1,0:T(8,128)S(1)}, f32[16,256]{1,0:T(8,128)}, u32[]{:S(2)}) copy-start(f32[16,256]{1,0:T(8,128)} %param.14) | copy-start | bytes 49156
  26.6 3.4 collective-permute-start.4
  27.3 3.0 collective-permute-start.5
  30.4 6.4 %collective-permute-start.6 = (f32[4,18,1]{2,1,0:T(8,128)S(1)}, f32[4,18,1]{2,1,0:T(8,128)S(1)}, u32[]{:S(2)}, u32[]{:S(2)}) collective-permute-start(f32[4,18,1]{2,1,0:T(8,128)S(1)} %get-tuple-element.29), channel_id=1, source_target_pairs={{0,1},{1,2},{2,3},{3,4},{4,5},{5,6},{6,7},{7,8},{8,9},{9,10},{10,1... | collective-permute-start | bytes 872 | tf_op jit(solution)/shard_map/ppermute | solution.py:20
  30.5 6.4 %collective-permute-start.7 = (f32[4,18,1]{2,1,0:T(8,128)S(1)}, f32[4,18,1]{2,1,0:T(8,128)S(1)}, u32[]{:S(2)}, u32[]{:S(2)}) collective-permute-start(f32[4,18,1]{2,1,0:T(8,128)S(1)} %get-tuple-element.30), channel_id=1, source_target_pairs={{1,0},{2,1},{3,2},{4,3},{5,4},{6,5},{7,6},{8,7},{9,8},{10,9},{11,1... | collective-permute-start | bytes 872 | tf_op jit(solution)/shard_map/ppermute | solution.py:21
  120.4 1.7 collective-permute-start.8
  120.4 3.0 collective-permute-start.9
  123.5 5.9 %collective-permute-start.10 = (f32[1,18,1]{2,1,0:T(8,128)S(1)}, f32[1,18,1]{2,1,0:T(8,128)S(1)}, u32[]{:S(2)}, u32[]{:S(2)}) collective-permute-start(f32[1,18,1]{2,1,0:T(8,128)S(1)} %get-tuple-element.35), channel_id=1, source_target_pairs={{0,1},{1,2},{2,3},{3,4},{4,5},{5,6},{6,7},{7,8},{8,9},{9,10},{10,1... | collective-permute-start | bytes 224 | tf_op jit(solution)/shard_map/ppermute | solution.py:20
  123.5 5.9 %collective-permute-start.11 = (f32[1,18,1]{2,1,0:T(8,128)S(1)}, f32[1,18,1]{2,1,0:T(8,128)S(1)}, u32[]{:S(2)}, u32[]{:S(2)}) collective-permute-start(f32[1,18,1]{2,1,0:T(8,128)S(1)} %get-tuple-element.36), channel_id=1, source_target_pairs={{1,0},{2,1},{3,2},{4,3},{5,4},{6,5},{7,6},{8,7},{9,8},{10,9},{11,1... | collective-permute-start | bytes 224 | tf_op jit(solution)/shard_map/ppermute | solution.py:21
  337.5 1.3 collective-permute-start.12
  337.5 3.0 collective-permute-start.13
  340.6 5.9 %collective-permute-start.14 = (f32[1,18,1]{2,1,0:T(8,128)S(1)}, f32[1,18,1]{2,1,0:T(8,128)S(1)}, u32[]{:S(2)}, u32[]{:S(2)}) collective-permute-start(f32[1,18,1]{2,1,0:T(8,128)S(1)} %get-tuple-element.33), channel_id=1, source_target_pairs={{0,1},{1,2},{2,3},{3,4},{4,5},{5,6},{6,7},{7,8},{8,9},{9,10},{10,1... | collective-permute-start | bytes 224 | tf_op jit(solution)/shard_map/ppermute | solution.py:20
  341.2 5.3 %collective-permute-start.15 = (f32[1,18,1]{2,1,0:T(8,128)S(1)}, f32[1,18,1]{2,1,0:T(8,128)S(1)}, u32[]{:S(2)}, u32[]{:S(2)}) collective-permute-start(f32[1,18,1]{2,1,0:T(8,128)S(1)} %get-tuple-element.34), channel_id=1, source_target_pairs={{1,0},{2,1},{3,2},{4,3},{5,4},{6,5},{7,6},{8,7},{9,8},{10,9},{11,1... | collective-permute-start | bytes 224 | tf_op jit(solution)/shard_map/ppermute | solution.py:21
